TPU v7x, 256 devices: a whole 4x4x8 slice. The times are simulated.
256 devices in a mesh: space: 64 (over z, y, core), rhs: 4 (over x).
Axes of the slice: x: 4, y: 4, z: 8, core: 2. Of those that a mesh axis runs over, the one named last changes fastest.
Arguments:
- rhs_vec: float32 [64, 65536], P('rhs', 'space'), may hold values from -40 to 40
- self_coef: float32 [65536], P('space'), may hold values from 2 to 4
- near_mats: bfloat16 [512, 8, 128, 128], P('space'), may hold values from -0.1875 to 0.1875
- near_ids: int32 [512, 8], P('space'), may hold values from 0 to 511, as said below
- near_count: int32 [512], P('space'), may hold values from 3 to 8, as said below
- interp: bfloat16 [512, 128, 32], P('space'), may hold values from -0.5 to 0.5
- skel_idx: int32 [512, 32], P('space'), may hold values from 0 to 127, as said below
- coupling: bfloat16 [16384, 4, 4096], P('space', 'rhs'), may hold values from -0.0234375 to 0.0234375
- diag_prec: float32 [65536], P('space'), may hold values from 1.5 to 4
- low_rank: float32 [65536, 512], P('space'), may hold values from -0.010481569 to 0.010481569
Outputs:
- solution: float32 [64, 65536], P('rhs', 'space')
Inputs may be any that keep to these rules, and one draw needn't show every extreme that they name: `near_ids`: slot 0 of each block names the block itself, slot 1 a block of the region before it (of its own region for the first region), slot 2 a block of the region after it (of its own region for the last region); every entry names a block of the same 8-block region or of the region before or after it. `near_count`: some regions use all 8 slots in every block. `skel_idx`: each row holds 32 distinct panel numbers of its block, rising.
All inputs are finite; a program needn't handle non-finite values.
Results may differ from a plain program's by a relative error of at most 0.001.
Values may be sent and summed in bfloat16 or wider, within the bound.
A program may use at most 64 MiB of HBM per device.

v0:
```python
import jax
import jax.numpy as jnp
from jax import lax
from jax.sharding import PartitionSpec as P

HIGH = lax.Precision.HIGHEST
EPS = 1e-06


def padded(cells, sides, width):
    for axis, dim in sides:
        count = lax.axis_size(axis)
        ends = count - 1
        head = lax.slice_in_dim(cells, 0, width, axis=dim)
        tail = lax.slice_in_dim(cells, cells.shape[dim] - width, cells.shape[dim], axis=dim)
        cells = jnp.concatenate(
            [
                lax.ppermute(tail, axis, [(i, (i + 1) % count) for i in range(ends)]),
                cells,
                lax.ppermute(head, axis, [((i + 1) % count, i) for i in range(ends)]),
            ],
            axis=dim,
        )
    return cells


def givens_pair(start_len, diag_one, below_one, upper_two, diag_two, below_two):
    radius_one = jnp.sqrt(diag_one * diag_one + below_one * below_one)
    cos_one = diag_one / radius_one
    sin_one = below_one / radius_one
    upper = cos_one * upper_two + sin_one * diag_two
    lower = cos_one * diag_two - sin_one * upper_two
    radius_two = jnp.sqrt(lower * lower + below_two * below_two)
    step_two = lower / radius_two * (-sin_one * start_len) / radius_two
    step_one = (cos_one * start_len - upper * step_two) / radius_one
    return (step_one, step_two)


def column_sum(values):
    return jnp.sum(values, axis=1)


def on_device(
    rhs_vec,
    self_coef,
    near_mats,
    near_ids,
    near_count,
    interp,
    skel_idx,
    coupling,
    diag_prec,
    low_rank,
):
    excitations, panels = rhs_vec.shape
    block_count, slot_count, block_width, _ = near_mats.shape
    skel_rank = interp.shape[2]
    quarters = lax.axis_size("rhs")
    quarter_len = skel_rank * block_count // quarters
    region = lax.axis_index("space")
    onehot = (
        skel_idx[:, :, None] == jnp.arange(block_width, dtype=jnp.int32)[None, None, :]
    ).astype(jnp.float32)
    restrict = onehot + jnp.swapaxes(interp.astype(jnp.float32), 1, 2)
    local_ids = near_ids - (region - 1) * block_count
    live_slots = jnp.arange(slot_count, dtype=jnp.int32)[None, :] < near_count[:, None]
    full_rows = lax.all_gather(coupling, "rhs", axis=1, tiled=True)

    def precond(vector):
        projected = lax.psum(jnp.dot(vector, low_rank, precision=HIGH), "space")
        return diag_prec[None, :] * vector - jnp.dot(projected, low_rank.T, precision=HIGH)

    def operate(field):
        field_low = field.astype(jnp.bfloat16)
        extended = padded(field_low, (("space", 1),), panels)
        blocks = extended.reshape(excitations, 3 * block_count, block_width)
        picked = blocks[:, local_ids] * live_slots[None, :, :, None].astype(jnp.bfloat16)
        near = jnp.einsum("bkij,ebkj->ebi", near_mats, picked, preferred_element_type=jnp.float32)
        own_blocks = field_low.reshape(excitations, block_count, block_width).astype(jnp.float32)
        charges = jnp.einsum("brj,ebj->ebr", restrict, own_blocks, precision=HIGH)
        packed = charges.astype(jnp.bfloat16).reshape(excitations, quarters, quarter_len)
        charges_in = lax.all_gather(packed, "space", axis=2, tiled=True)
        far_field = jnp.einsum(
            "sqc,eqc->es", full_rows, charges_in, preferred_element_type=jnp.float32
        )
        far_pot = jnp.einsum(
            "brj,ebr->ebj",
            restrict,
            far_field.reshape(excitations, block_count, skel_rank),
            precision=HIGH,
        )
        return (
            self_coef[None, :] * field
            + near.reshape(excitations, panels)
            + far_pot.reshape(excitations, panels)
        )

    def orthogonalize(residue, basis_vecs):
        coeffs = lax.psum(
            jnp.stack([column_sum(residue * basis_one) for basis_one in basis_vecs]), "space"
        )
        for index_one in range(len(basis_vecs)):
            residue = residue - coeffs[index_one][:, None] * basis_vecs[index_one]
        length = jnp.sqrt(lax.psum(column_sum(residue * residue), "space") + EPS)
        return (residue, coeffs, length)

    start_len = jnp.sqrt(lax.psum(column_sum(rhs_vec * rhs_vec), "space") + EPS)
    first_dir = rhs_vec / start_len[:, None]
    first_pre = precond(first_dir)
    residue, coeffs_one, below_one = orthogonalize(operate(first_pre), [first_dir])
    second_dir = residue / below_one[:, None]
    second_pre = precond(second_dir)
    residue, coeffs_two, below_two = orthogonalize(operate(second_pre), [first_dir, second_dir])
    step_one, step_two = givens_pair(
        start_len, coeffs_one[0], below_one, coeffs_two[0], coeffs_two[1], below_two
    )
    return step_one[:, None] * first_pre + step_two[:, None] * second_pre


def solution(mesh):
    placed = (
        P("rhs", "space"),
        P("space"),
        P("space", None, None, None),
        P("space", None),
        P("space"),
        P("space", None, None),
        P("space", None),
        P("space", "rhs", None),
        P("space"),
        P("space", None),
    )
    return jax.shard_map(
        on_device, mesh=mesh, in_specs=placed, out_specs=P("rhs", "space"), check_vma=False
    )
```

profile of v0, /device:TPU:1, one launch (start us, length us, event | category | flops | bytes accessed | tf_op | source)
XLA Modules:
  0.0 1282.3 jit_solution(1113078736265904027)
XLA Ops:
  6.5 0.7 all-gather.2.cloned.1.call-update
  7.3 0.3 copy-done.1
  7.6 128.3 %psum.49 = f32[16]{0:T(128)S(1)} all-reduce(f32[16]{0:T(128)S(1)} %multiply_reduce_fusion.5), channel_id=1, replica_groups=mesh['space'=64,'rhs'=4] {'space'}, use_global_device_ids=true, to_apply=%region_1.0 | all-reduce | flops 16 | bytes 128 | tf_op jit(solution)/shard_map/psum | solution.py:107
  136.0 1.1 fusion.30
  137.1 245.5 %psum.50 = f32[16,512]{1,0:T(8,128)S(1)} all-reduce(f32[16,512]{1,0:T(8,128)S(1)} %fusion.30), channel_id=1, replica_groups=mesh['space'=64,'rhs'=4] {'space'}, use_global_device_ids=true, to_apply=%region_2.0 | all-reduce | flops 8192 | bytes 65536 | tf_op jit(solution)/shard_map/psum | solution.py:70
  382.6 1.8 fusion.31
  384.4 7.6 collective-permute-start.1
  392.0 1.9 collective-permute-start
  393.9 0.3 fusion.4
  394.6 54.5 %all_gather.9 = bf16[16,4,4096]{0,1,2:T(4,128)(2,1)} all-gather(bf16[16,4,64]{0,1,2:T(4,128)(2,1)S(1)} %copy.39), channel_id=1, replica_groups=mesh['space'=64,'rhs'=4] {'space'}, dimensions={2}, use_global_device_ids=true | all-gather | bytes 532480 | tf_op jit(solution)/shard_map/all_gather | solution.py:82
  449.1 0.6 gather_fusion
  449.8 2.3 convolution_bitcast_fusion.3
  452.1 6.9 fusion.6
  459.1 0.3 convolution_bitcast_fusion.1
  459.6 123.6 %psum.51 = f32[16]{0:T(128)S(1)} all-reduce(f32[16]{0:T(128)S(1)} %get-tuple-element.10), channel_id=1, replica_groups=mesh['space'=64,'rhs'=4] {'space'}, use_global_device_ids=true, to_apply=%region_4.0 | all-reduce | flops 16 | bytes 128 | tf_op jit(solution)/shard_map/psum | solution.py:99
  583.4 126.7 %psum.52 = f32[16]{0:T(128)S(1)} all-reduce(f32[16]{0:T(128)S(1)} %multiply_reduce_fusion.3), channel_id=1, replica_groups=mesh['space'=64,'rhs'=4] {'space'}, use_global_device_ids=true, to_apply=%region_6.0 | all-reduce | flops 16 | bytes 128 | tf_op jit(solution)/shard_map/psum | solution.py:104
  710.2 1.1 fusion.33
  711.3 241.3 %psum.53 = f32[16,512]{1,0:T(8,128)S(1)} all-reduce(f32[16,512]{1,0:T(8,128)S(1)} %fusion.33), channel_id=1, replica_groups=mesh['space'=64,'rhs'=4] {'space'}, use_global_device_ids=true, to_apply=%region_7.0 | all-reduce | flops 8192 | bytes 65536 | tf_op jit(solution)/shard_map/psum | solution.py:70
  952.6 1.8 fusion.32
  954.4 0.3 fusion.5
  954.7 7.6 collective-permute-start.3
  962.3 1.9 collective-permute-start.2
  964.4 50.4 %all_gather.11 = bf16[16,4,4096]{0,1,2:T(4,128)(2,1)S(1)} all-gather(bf16[16,4,64]{0,1,2:T(4,128)(2,1)S(1)} %copy.47), channel_id=1, replica_groups=mesh['space'=64,'rhs'=4] {'space'}, dimensions={2}, use_global_device_ids=true | all-gather | bytes 532480 | tf_op jit(solution)/shard_map/all_gather | solution.py:82
  1014.9 5.8 fusion.9
  1020.7 0.3 convolution_bitcast_fusion
  1021.1 0.6 gather_fusion.1
  1021.7 2.3 convolution_bitcast_fusion.2
  1024.0 0.2 multiply_reduce_fusion.2
  1024.2 123.6 %psum.54 = f32[2,16]{1,0:T(2,128)S(1)} all-reduce(f32[2,16]{1,0:T(2,128)S(1)} %pad_maximum_fusion), channel_id=1, replica_groups=mesh['space'=64,'rhs'=4] {'space'}, use_global_device_ids=true, to_apply=%region_10.0 | all-reduce | flops 32 | bytes 256 | tf_op jit(solution)/shard_map/psum | solution.py:99
  1147.8 0.2 multiply_reduce_fusion
  1148.0 126.7 %psum.55 = f32[16]{0:T(128)S(1)} all-reduce(f32[16]{0:T(128)S(1)} %multiply_reduce_fusion), channel_id=1, replica_groups=mesh['space'=64,'rhs'=4] {'space'}, use_global_device_ids=true, to_apply=%region_12.0 | all-reduce | flops 16 | bytes 128 | tf_op jit(solution)/shard_map/psum | solution.py:104
  1274.7 0.7 multiply_add_fusion
  (44 shorter events, 1.6 us)
Async XLA Ops:
  6.5 129.4 %copy-start = (f32[1024,512]{1,0:T(8,128)S(1)}, f32[1024,512]{1,0:T(8,128)}, u32[]{:S(2)}) copy-start(f32[1024,512]{1,0:T(8,128)} %param.19) | copy-start | bytes 6291460
  6.5 1.0 copy-start.1
  6.5 376.0 %copy-start.3 = (f32[1024]{0:T(1024)S(1)}, f32[1024]{0:T(1024)}, u32[]{:S(2)}) copy-start(f32[1024]{0:T(1024)} %param.18) | copy-start | bytes 12292
  6.5 445.5 %all-gather.2.cloned.1.call-start = ((), (), s32[]{:S(2)}) async-start(), calls=%async_computation | async-start | bytes 10485760 | tf_op jit(solution)/shard_map/all_gather | solution.py:67
  135.9 258.0 %copy-start.2 = (bf16[8,128,32]{1,2,0:T(8,128)(2,1)S(1)}, bf16[8,128,32]{1,2,0:T(8,128)(2,1)}, u32[]{:S(2)}) copy-start(bf16[8,128,32]{1,2,0:T(8,128)(2,1)} %param.15) | copy-start | bytes 196612
  135.9 258.0 %copy-start.4 = (s32[8,32]{1,0:T(8,128)S(1)}, s32[8,32]{1,0:T(8,128)}, u32[]{:S(2)}) copy-start(s32[8,32]{1,0:T(8,128)} %param.16) | copy-start | bytes 3076
  135.9 258.5 %copy-start.6 = (s32[8,8]{1,0:T(8,128)S(1)}, s32[8,8]{1,0:T(8,128)}, u32[]{:S(2)}) copy-start(s32[8,8]{1,0:T(8,128)} %param.13) | copy-start | bytes 772
  384.4 64.7 %collective-permute-start.1 = (bf16[16,1024]{1,0:T(8,128)(2,1)S(1)}, bf16[16,1024]{1,0:T(8,128)(2,1)S(1)}, u32[]{:S(2)}, u32[]{:S(2)}) collective-permute-start(bf16[16,1024]{1,0:T(8,128)(2,1)S(1)} %get-tuple-element.14), channel_id=1, source_target_pairs={{4,0},{8,4},{12,8},{16,12},{20,16},{24,20},{28,24},{32,28},{36,32}... | collective-permute-start | bytes 98312 | tf_op jit(solution)/shard_map/ppermute | solution.py:20
  392.0 57.2 %collective-permute-start = (bf16[16,1024]{1,0:T(8,128)(2,1)S(1)}, bf16[16,1024]{1,0:T(8,128)(2,1)S(1)}, u32[]{:S(2)}, u32[]{:S(2)}) collective-permute-start(bf16[16,1024]{1,0:T(8,128)(2,1)S(1)} %get-tuple-element.14), channel_id=1, source_target_pairs={{0,4},{4,8},{8,12},{12,16},{16,20},{20,24},{24,28},{28,32},{32,36}... | collective-permute-start | bytes 98312 | tf_op jit(solution)/shard_map/ppermute | solution.py:18
  394.6 54.5 %copy-start.7 = (s32[8]{0:T(128)S(1)}, s32[8]{0:T(128)}, u32[]{:S(2)}) copy-start(s32[8]{0:T(128)} %param.14) | copy-start | bytes 100
  452.1 7.4 copy-start.5
  954.7 66.3 %collective-permute-start.3 = (bf16[16,1024]{1,0:T(8,128)(2,1)S(1)}, bf16[16,1024]{1,0:T(8,128)(2,1)S(1)}, u32[]{:S(2)}, u32[]{:S(2)}) collective-permute-start(bf16[16,1024]{1,0:T(8,128)(2,1)S(1)} %get-tuple-element.16), channel_id=1, source_target_pairs={{4,0},{8,4},{12,8},{16,12},{20,16},{24,20},{28,24},{32,28},{36,32}... | collective-permute-start | bytes 98312 | tf_op jit(solution)/shard_map/ppermute | solution.py:20
  962.3 58.8 %collective-permute-start.2 = (bf16[16,1024]{1,0:T(8,128)(2,1)S(1)}, bf16[16,1024]{1,0:T(8,128)(2,1)S(1)}, u32[]{:S(2)}, u32[]{:S(2)}) collective-permute-start(bf16[16,1024]{1,0:T(8,128)(2,1)S(1)} %get-tuple-element.16), channel_id=1, source_target_pairs={{0,4},{4,8},{8,12},{12,16},{16,20},{20,24},{24,28},{28,32},{32,36}... | collective-permute-start | bytes 98312 | tf_op jit(solution)/shard_map/ppermute | solution.py:18
Sparse Core Ops, SparseCore 0:
  9.2 89.4 all-gather.1
where the time goes:
time: 1280 us
  blocking collectives  1220 us (95%)
  matrix products  24.4 us (2%)
  starting transfers between devices  19 us (1%)
  between operations  13.6 us (1%)
    psum x2, blocking collectives, precond(): projected = lax.psum(jnp.dot(vector, low_rank, precision=HIGH), 'space')  487 us
    psum x2, blocking collectives, orthogonalize(): length = jnp.sqrt(lax.psum(column_sum(residue * residue), 'space') + EPS)  253 us
    psum x2, blocking collectives, orthogonalize(): lax.psum(jnp.stack([column_sum(residue * basis_one) for basis_one in basi...  247 us
    psum x1, blocking collectives, on_device(): start_len = jnp.sqrt(lax.psum(column_sum(rhs_vec * rhs_vec), 'space') + EPS)  128 us
    all_gather x2, blocking collectives, operate(): charges_in = lax.all_gather(packed, 'space', axis=2, tiled=True)  105 us
  transfers between devices with their start and end apart: 5, of which 0 were waited for; matrix products, arithmetic and copies ran while one was open for 1% of the time, Pallas kernels for 0%

commit v1 on v0

--- a/solution.py
+++ b/solution.py
@@ -79,7 +79,9 @@
         own_blocks = field_low.reshape(excitations, block_count, block_width).astype(jnp.float32)
         charges = jnp.einsum("brj,ebj->ebr", restrict, own_blocks, precision=HIGH)
         packed = charges.astype(jnp.bfloat16).reshape(excitations, quarters, quarter_len)
-        charges_in = lax.all_gather(packed, "space", axis=2, tiled=True)
+        charges_in = jnp.concatenate(
+            lax.all_to_all(jnp.stack([packed] * lax.axis_size("space")), "space", 0, 0), axis=2
+        )
         far_field = jnp.einsum(
             "sqc,eqc->es", full_rows, charges_in, preferred_element_type=jnp.float32
         )

time: 1280 us -> 1230 us (0.961)
  blocking collectives: 1220 us -> 1110 us
  waiting for transfers between devices: 0.72 us -> 19 us
  starting transfers between devices: 19 us -> 36.1 us
  local copies, waits for them, and re-layouts: 2.29 us -> 15.3 us
    all_gather x2 -> x0, blocking collectives: 105 us -> none  [operate(): charges_in = lax.all_gather(packed, 'space', axis=2, tiled=True)]
    all_to_all x0 -> x2, starting transfers between devices: none -> 24.8 us  [operate(): lax.all_to_all(jnp.stack([packed] * lax.axis_size('space')), 'space', 0, 0)]
    all_to_all x0 -> x2, waiting for transfers between devices: none -> 16.6 us  [operate(): lax.all_to_all(jnp.stack([packed] * lax.axis_size('space')), 'space', 0, 0)]
  transfers between devices with their start and end apart: 5 -> 7, of which waited for: 0 -> 5; matrix products, arithmetic and copies ran while one was open for 1% -> 1% of each run, Pallas kernels for 0% -> 0%
where the time goes in v1:
time: 1230 us
  blocking collectives  1110 us (90%)
  starting transfers between devices  36.1 us (3%)
  matrix products  29.8 us (2%)
  waiting for transfers between devices  19 us (2%)
  local copies, waits for them, and re-layouts  15.3 us (1%)
  between operations  13.7 us (1%)
    psum x2, blocking collectives, precond(): projected = lax.psum(jnp.dot(vector, low_rank, precision=HIGH), 'space')  487 us
    psum x2, blocking collectives, orthogonalize(): length = jnp.sqrt(lax.psum(column_sum(residue * residue), 'space') + EPS)  252 us
    psum x2, blocking collectives, orthogonalize(): lax.psum(jnp.stack([column_sum(residue * basis_one) for basis_one in basi...  247 us
    psum x1, blocking collectives, on_device(): start_len = jnp.sqrt(lax.psum(column_sum(rhs_vec * rhs_vec), 'space') + EPS)  128 us
    all_to_all x2, starting transfers between devices, operate(): lax.all_to_all(jnp.stack([packed] * lax.axis_size('space')), 'space', 0, 0)  24.8 us
  transfers between devices with their start and end apart: 7, of which 5 were waited for; matrix products, arithmetic and copies ran while one was open for 1% of the time, Pallas kernels for 0%

profile of v1, /device:TPU:1, one launch (start us, length us, event | category | flops | bytes accessed | tf_op | source)
XLA Modules:
  0.0 1229.7 jit_solution(389475474566951855)
XLA Ops:
  6.5 0.7 all-gather.2.cloned.1.call-update
  7.6 128.3 %psum.49 = f32[16]{0:T(128)S(1)} all-reduce(f32[16]{0:T(128)S(1)} %multiply_reduce_fusion.5), channel_id=1, replica_groups=mesh['space'=64,'rhs'=4] {'space'}, use_global_device_ids=true, to_apply=%region_1.0 | all-reduce | flops 16 | bytes 128 | tf_op jit(solution)/shard_map/psum | solution.py:109
  136.0 1.1 fusion.20
  137.1 245.5 %psum.50 = f32[16,512]{1,0:T(8,128)S(1)} all-reduce(f32[16,512]{1,0:T(8,128)S(1)} %fusion.20), channel_id=1, replica_groups=mesh['space'=64,'rhs'=4] {'space'}, use_global_device_ids=true, to_apply=%region_2.0 | all-reduce | flops 8192 | bytes 65536 | tf_op jit(solution)/shard_map/psum | solution.py:70
  382.6 1.8 fusion.21
  385.1 1.6 reshape.118
  386.7 10.5 all-to-all-start
  397.3 2.5 collective-permute-start.1
  399.8 3.2 collective-permute-start
  404.5 2.3 convolution_bitcast_fusion.5
  406.8 8.4 all-to-all-done
  415.1 2.3 reshape.119
  417.6 0.7 copy.50
  418.3 1.7 reshape.111
  420.0 9.1 convolution_bitcast_fusion.1
  429.6 123.7 %psum.51 = f32[16]{0:T(128)S(1)} all-reduce(f32[16]{0:T(128)S(1)} %get-tuple-element.10), channel_id=1, replica_groups=mesh['space'=64,'rhs'=4] {'space'}, use_global_device_ids=true, to_apply=%region_4.0 | all-reduce | flops 16 | bytes 128 | tf_op jit(solution)/shard_map/psum | solution.py:101
  553.5 125.8 %psum.52 = f32[16]{0:T(128)S(1)} all-reduce(f32[16]{0:T(128)S(1)} %multiply_reduce_fusion.3), channel_id=1, replica_groups=mesh['space'=64,'rhs'=4] {'space'}, use_global_device_ids=true, to_apply=%region_6.0 | all-reduce | flops 16 | bytes 128 | tf_op jit(solution)/shard_map/psum | solution.py:106
  679.4 1.1 fusion.23
  680.5 241.1 %psum.53 = f32[16,512]{1,0:T(8,128)S(1)} all-reduce(f32[16,512]{1,0:T(8,128)S(1)} %fusion.23), channel_id=1, replica_groups=mesh['space'=64,'rhs'=4] {'space'}, use_global_device_ids=true, to_apply=%region_7.0 | all-reduce | flops 8192 | bytes 65536 | tf_op jit(solution)/shard_map/psum | solution.py:70
  921.6 1.8 fusion.22
  924.1 1.6 reshape.120
  925.8 14.3 %all-to-all-start.1 = ((bf16[64,2,2048]{2,1,0:T(2,128)(2,1)}), bf16[64,2,2048]{2,1,0:T(2,128)(2,1)}, u32[]{:S(2)}, u32[]{:S(2)}) async-start(bf16[64,2,2048]{2,1,0:T(2,128)(2,1)} %reshape.120), calls=%async_computation.1 | async-start | bytes 1048576 | tf_op jit(solution)/shard_map/all_to_all | solution.py:83
  940.1 2.4 collective-permute-start.3
  942.5 3.1 collective-permute-start.2
  947.3 2.3 convolution_bitcast_fusion.4
  949.6 8.3 all-to-all-done.1
  957.8 2.3 reshape.121
  961.0 1.7 reshape.114
  962.7 9.1 convolution_bitcast_fusion
  972.3 123.7 %psum.54 = f32[2,16]{1,0:T(2,128)S(1)} all-reduce(f32[2,16]{1,0:T(2,128)S(1)} %pad_maximum_fusion), channel_id=1, replica_groups=mesh['space'=64,'rhs'=4] {'space'}, use_global_device_ids=true, to_apply=%region_10.0 | all-reduce | flops 32 | bytes 256 | tf_op jit(solution)/shard_map/psum | solution.py:101
  1096.2 125.8 %psum.55 = f32[16]{0:T(128)S(1)} all-reduce(f32[16]{0:T(128)S(1)} %multiply_reduce_fusion), channel_id=1, replica_groups=mesh['space'=64,'rhs'=4] {'space'}, use_global_device_ids=true, to_apply=%region_12.0 | all-reduce | flops 16 | bytes 128 | tf_op jit(solution)/shard_map/psum | solution.py:106
  1222.1 0.7 multiply_add_fusion
  (68 shorter events, 7.5 us)
Async XLA Ops:
  6.5 129.4 %copy-start = (f32[1024,512]{1,0:T(8,128)S(1)}, f32[1024,512]{1,0:T(8,128)}, u32[]{:S(2)}) copy-start(f32[1024,512]{1,0:T(8,128)} %param.19) | copy-start | bytes 6291460
  6.5 1.0 copy-start.1
  6.5 376.0 %copy-start.3 = (f32[1024]{0:T(1024)S(1)}, f32[1024]{0:T(1024)}, u32[]{:S(2)}) copy-start(f32[1024]{0:T(1024)} %param.18) | copy-start | bytes 12292
  6.5 413.4 %all-gather.2.cloned.1.call-start = ((), (), s32[]{:S(2)}) async-start(), calls=%async_computation.2 | async-start | bytes 10485760 | tf_op jit(solution)/shard_map/all_gather | solution.py:67
  135.9 248.5 %copy-start.10 = (f32[16]{0:T(128)}, f32[16]{0:T(128)S(1)}, u32[]{:S(2)}) copy-start(f32[16]{0:T(128)S(1)} %psum.49) | copy-start | bytes 196
  135.9 248.5 %copy-start.2 = (bf16[8,128,32]{1,2,0:T(8,128)(2,1)S(1)}, bf16[8,128,32]{1,2,0:T(8,128)(2,1)}, u32[]{:S(2)}) copy-start(bf16[8,128,32]{1,2,0:T(8,128)(2,1)} %param.15) | copy-start | bytes 196612
  135.9 248.5 %copy-start.4 = (s32[8,32]{1,0:T(8,128)S(1)}, s32[8,32]{1,0:T(8,128)}, u32[]{:S(2)}) copy-start(s32[8,32]{1,0:T(8,128)} %param.16) | copy-start | bytes 3076
  384.4 18.6 %copy-start.8 = (s32[8,8]{1,0:T(8,128)S(1)}, s32[8,8]{1,0:T(8,128)}, u32[]{:S(2)}) copy-start(s32[8,8]{1,0:T(8,128)} %param.13) | copy-start | bytes 772
  384.4 18.7 %copy-start.9 = (s32[8]{0:T(128)S(1)}, s32[8]{0:T(128)}, u32[]{:S(2)}) copy-start(s32[8]{0:T(128)} %param.14) | copy-start | bytes 100
  386.7 28.4 %all-to-all-start = ((bf16[64,2,2048]{2,1,0:T(2,128)(2,1)}), bf16[64,2,2048]{2,1,0:T(2,128)(2,1)}, u32[]{:S(2)}, u32[]{:S(2)}) async-start(bf16[64,2,2048]{2,1,0:T(2,128)(2,1)} %reshape.118), calls=%async_computation | async-start | bytes 1048576 | tf_op jit(solution)/shard_map/all_to_all | solution.py:83
  397.3 5.9 collective-permute-start.1
  399.8 4.0 collective-permute-start
  420.0 9.4 copy-start.5
  553.3 370.2 %copy-start.6 = (f32[16]{0:T(128)}, f32[16]{0:T(128)S(1)}, u32[]{:S(2)}) copy-start(f32[16]{0:T(128)S(1)} %psum.51) | copy-start | bytes 196
  679.3 244.2 %copy-start.12 = (f32[16]{0:T(128)}, f32[16]{0:T(128)S(1)}, u32[]{:S(2)}) copy-start(f32[16]{0:T(128)S(1)} %psum.52) | copy-start | bytes 196
  925.8 32.1 %all-to-all-start.1 = ((bf16[64,2,2048]{2,1,0:T(2,128)(2,1)}), bf16[64,2,2048]{2,1,0:T(2,128)(2,1)}, u32[]{:S(2)}, u32[]{:S(2)}) async-start(bf16[64,2,2048]{2,1,0:T(2,128)(2,1)} %reshape.120), calls=%async_computation.1 | async-start | bytes 1048576 | tf_op jit(solution)/shard_map/all_to_all | solution.py:83
  940.1 6.0 collective-permute-start.3
  942.5 4.1 collective-permute-start.2
  962.7 259.4 %copy-start.7 = (f32[16]{0:T(128)S(1)}, f32[16]{0:T(128)}, u32[]{:S(2)}) copy-start(f32[16]{0:T(128)} %copy-done.6) | copy-start | bytes 196
  962.7 259.4 %copy-start.11 = (f32[16]{0:T(128)S(1)}, f32[16]{0:T(128)}, u32[]{:S(2)}) copy-start(f32[16]{0:T(128)} %copy-done.10) | copy-start | bytes 196
  962.7 259.4 %copy-start.13 = (f32[16]{0:T(128)S(1)}, f32[16]{0:T(128)}, u32[]{:S(2)}) copy-start(f32[16]{0:T(128)} %copy-done.12) | copy-start | bytes 196
Sparse Core Ops, SparseCore 0:
  9.2 89.4 all-gather.1
